TPU v7x, 32 devices: a whole 2x2x4 slice. The times are simulated.
32 devices in a mesh: groups: 2 (over y), expert: 4 (over z), tensor: 2 (over x), inner: 2 (over core).
Axes of the slice: x: 2, y: 2, z: 4, core: 2. Of those that a mesh axis runs over, the one named last changes fastest.
Arguments:
- tokens: bfloat16 [1024, 7168], P(('groups', 'expert'), ('tensor', 'inner')), parts along dimension 0, may hold values from -6 to 6
- expert_ids: int32 [1024, 8], P(('groups', 'expert')), parts along dimension 0, may hold values from 0 to 31, all different within a row; in each aligned block of 128 rows (0 to 127, 128 to 255, ...) at most 96 rows name the same one
- gate_weights: float32 [1024, 8], P(('groups', 'expert')), parts along dimension 0, may hold values from 0.05 to 0.45
- base_weights: bfloat16 [3, 1024, 7168], P(None, 'expert', ('tensor', 'inner')), may hold values from -0.0625 to 0.0625
- in_factor: bfloat16 [3840, 7168], P('expert', ('tensor', 'inner')), may hold values from -0.0625 to 0.0625
- out_factors: bfloat16 [2, 3840, 1024], P(None, 'expert', ('tensor', 'inner')), may hold values from -0.375 to 0.375
- ranks: int32 [32], P('expert'), may hold values from 64 to 512, as said below
Outputs:
- mixed: bfloat16 [1024, 7168], P(('groups', 'expert'), ('tensor', 'inner')), parts along dimension 0
There are 2 independent parts, one for each index of `groups`. A program takes and returns all parts, laid end to end along the dimension named above; an argument that names none is the same for every part. Nothing has to cross between parts.
Inputs may be any that keep to these rules, and one draw needn't show every extreme that they name: `expert_ids`: in each aligned block of 128 tokens no expert is chosen more than 96 times, and some expert is chosen exactly 96 times; the experts of one token differ. The ranks of each aligned block of 8 experts sum to exactly 960.
All inputs are finite; a program needn't handle non-finite values.
Results may differ from a plain program's by a relative error of at most 0.023.
Values may be sent and summed in bfloat16 or wider, within the bound.
No kernel may reach another device: no remote copies, remote signals or barrier semaphores. Data moves between devices by JAX's collectives and lax.ppermute only.
A program may use at most 64 MiB of HBM per device.

v0:
```python
import jax
import jax.numpy as jnp
from jax import lax
from jax.sharding import PartitionSpec as P

RANK_MAX = 512


def on_device(tokens, expert_ids, gate_weights, base_weights, in_factor, out_factors, ranks):
    tok_rows, feat_slice = tokens.shape
    top_count = expert_ids.shape[1]
    owners = lax.axis_size("expert")
    local_count = ranks.shape[0]
    experts = local_count * owners
    capacity = min(tok_rows, 3 * tok_rows * top_count // experts)
    hidden_slice = out_factors.shape[2]
    width = RANK_MAX
    gathered = lax.all_gather(base_weights, "expert", axis=1, tiled=True)
    partial_value = jnp.einsum(
        "td,gfd->tgf", tokens, gathered[:2], preferred_element_type=jnp.float32
    )
    base_rows = lax.psum_scatter(
        partial_value.astype(jnp.bfloat16), ("tensor", "inner"), scatter_dimension=2, tiled=True
    )
    pairs = tok_rows * top_count
    flat_ids = expert_ids.reshape(pairs)
    columns = lax.broadcasted_iota(jnp.int32, (pairs, experts), 1)
    onehot = (flat_ids[:, None] == columns).astype(jnp.bfloat16)
    row_pos = lax.broadcasted_iota(jnp.int32, (pairs, pairs), 0)
    col_pos = lax.broadcasted_iota(jnp.int32, (pairs, pairs), 1)
    earlier = (row_pos > col_pos).astype(jnp.bfloat16)
    counts = jnp.dot(earlier, onehot, preferred_element_type=jnp.float32)
    slot = jnp.sum(counts * onehot.astype(jnp.float32), axis=1).astype(jnp.int32)
    owner_of = flat_ids // local_count
    member_of = flat_ids % local_count
    target = (member_of * owners + owner_of) * capacity + slot
    source_row = lax.broadcasted_iota(jnp.int32, (pairs,), 0) // top_count
    outgoing = jnp.zeros((local_count * owners * capacity, feat_slice), jnp.bfloat16)
    outgoing = outgoing.at[target].set(tokens[source_row])
    outgoing = outgoing.reshape(local_count, owners, capacity, feat_slice)
    arrived = lax.all_to_all(outgoing, "expert", split_axis=1, concat_axis=1, tiled=True)
    slots = owners * capacity
    arrived = arrived.reshape(local_count, slots, feat_slice)
    starts = jnp.cumsum(ranks) - ranks
    in_pad = jnp.concatenate([in_factor, jnp.zeros((width, feat_slice), jnp.bfloat16)], 0)
    out_pad = jnp.concatenate([out_factors, jnp.zeros((2, width, hidden_slice), jnp.bfloat16)], 1)
    within = lax.broadcasted_iota(jnp.int32, (1, width), 1)
    terms = []
    for member in range(local_count):
        window = lax.dynamic_slice_in_dim(in_pad, starts[member], width, 0)
        terms.append(
            lax.dot_general(
                arrived[member],
                window,
                (((1,), (1,)), ((), ())),
                preferred_element_type=jnp.float32,
            )
        )
    stacked = jnp.stack(
        [
            jnp.where(within < ranks[member], terms[member], jnp.float32(0.0))
            for member in range(local_count)
        ]
    )
    summed = lax.psum(stacked.astype(jnp.bfloat16), ("tensor", "inner"))
    latents = [summed[member] for member in range(local_count)]
    outputs = []
    for member in range(local_count):
        factor = lax.dynamic_slice_in_dim(out_pad, starts[member], width, 1)
        outputs.append(
            jnp.einsum(
                "rc,gcf->rgf", latents[member], factor, preferred_element_type=jnp.float32
            ).astype(jnp.bfloat16)
        )
    replies = jnp.stack(outputs).reshape(local_count, owners, capacity, 2, hidden_slice)
    returned = lax.all_to_all(replies, "expert", split_axis=1, concat_axis=1, tiled=True)
    returned = returned.reshape(local_count * owners * capacity, 2, hidden_slice)
    delta = returned[target].reshape(tok_rows, top_count, 2, hidden_slice)
    summed_rows = base_rows.astype(jnp.float32)[:, None] + delta.astype(jnp.float32)
    hidden = (jax.nn.silu(summed_rows[:, :, 0]) * summed_rows[:, :, 1]).astype(jnp.bfloat16)
    combined = jnp.sum(gate_weights[:, :, None] * hidden.astype(jnp.float32), axis=1).astype(
        jnp.bfloat16
    )
    full_hidden = lax.all_gather(combined, ("tensor", "inner"), axis=1, tiled=True)
    return jnp.dot(full_hidden, gathered[2], preferred_element_type=jnp.float32).astype(
        jnp.bfloat16
    )


def solution(mesh):
    return jax.shard_map(
        on_device,
        mesh=mesh,
        in_specs=(
            P(("groups", "expert"), ("tensor", "inner")),
            P(("groups", "expert"), None),
            P(("groups", "expert"), None),
            P(None, "expert", ("tensor", "inner")),
            P("expert", ("tensor", "inner")),
            P(None, "expert", ("tensor", "inner")),
            P("expert"),
        ),
        out_specs=P(("groups", "expert"), ("tensor", "inner")),
        check_vma=False,
    )
```

profile of v0, /device:TPU:0, one launch (start us, length us, event | category | flops | bytes accessed | tf_op | source)
XLA Modules:
  0.0 655.1 jit_solution(18073991329550731420)
XLA Ops:
  7.4 0.8 copy.40
  8.4 0.5 fusion.52
  9.0 31.3 %scatter_custom_fusion = bf16[3072,1792]{1,0:T(8,128)(2,1)} fusion(s32[1024]{0:T(1024)S(1)} %bitcast.155, bf16[]{:T(256)} %constant.47.clone.1, bf16[128,1792]{1,0:T(8,128)(2,1)S(1)} %copy-done, s32[1024]{0:T(1024)S(1)} %broadcast_clamp_fusion.1), kind=kCustom, calls=%fused_computation.13 | custom fusion | bytes 11010050 | tf_op jit(solution)/shard_map/scatter | solution.py:39
  40.3 9.6 %copy.42 = bf16[8,4,96,1792]{3,2,0,1:T(8,128)(2,1)} copy(bf16[8,4,96,1792]{3,2,1,0:T(8,128)(2,1)} %bitcast.135) | data formatting | bytes 22020096 | tf_op jit(solution)/shard_map/reshape | solution.py:40
  50.0 6.5 all-to-all-start
  56.6 0.7 fusion.94
  72.4 0.7 fusion.93
  73.1 0.6 iota_compare_fusion.15
  73.8 0.6 iota_compare_fusion.14
  74.4 0.6 iota_compare_fusion.13
  75.0 0.7 iota_compare_fusion.12
  75.7 0.6 iota_compare_fusion.11
  76.2 0.7 iota_compare_fusion.10
  76.9 0.6 iota_compare_fusion.9
  77.6 0.7 iota_compare_fusion.8
  78.2 218.9 %all-to-all-done = bf16[8,4,96,1792]{3,2,0,1:T(8,128)(2,1)} async-done(((bf16[8,4,96,1792]{3,2,0,1:T(8,128)(2,1)}), bf16[8,4,96,1792]{3,2,0,1:T(8,128)(2,1)}, u32[]{:S(2)}, u32[]{:S(2)}) %all-to-all-start) | async-done | bytes 11010080 | tf_op jit(solution)/shard_map/all_to_all | solution.py:41
  297.2 4.9 fusion.91
  302.4 1.9 fusion.50
  304.3 1.9 fusion.48
  306.2 1.9 fusion.46
  308.1 1.9 fusion.44
  310.0 1.9 fusion.42
  311.9 1.9 fusion.40
  313.8 1.9 fusion.38
  315.7 1.9 fusion.36
  318.2 67.2 %all-reduce.4.cloned.1.call-done = bf16[8,384,512]{2,1,0:T(8,128)(2,1)} async-done(((bf16[8,384,512]{2,1,0:T(8,128)(2,1)}), bf16[8,384,512]{2,1,0:T(8,128)(2,1)}) %all-reduce.4.cloned.1.call-update) | async-done | bytes 3145744 | tf_op jit(solution)/shard_map/psum | solution.py:65
  385.4 1.6 convolution_convert_fusion.7
  387.1 1.5 convolution_convert_fusion.6
  388.7 0.5 convolution_convert_fusion.5
  389.2 0.5 convolution_convert_fusion.4
  389.8 0.5 convolution_convert_fusion.3
  390.3 0.5 convolution_convert_fusion.2
  390.9 0.5 convolution_convert_fusion.1
  391.4 0.5 convolution_convert_fusion
  392.0 1.9 copy.54
  393.9 4.7 all-to-all-start.1
  398.6 179.9 %all-gather.2.cloned.1.call-done = bf16[3,1024,1792]{2,1,0:T(8,128)(2,1)} async-done(((bf16[3,256,1792]{2,1,0:T(8,128)(2,1)}), bf16[3,1024,1792]{2,1,0:T(8,128)(2,1)}) %all-gather.2.cloned.1.call-update) | async-done | bytes 11010064 | tf_op jit(solution)/shard_map/all_gather | solution.py:18
  578.4 6.3 fusion.16
  584.9 19.8 %reduce-scatter.2.cloned.1.call-done = bf16[128,2,256]{2,0,1:T(8,128)(2,1)} async-done(((bf16[128,2,1024]{2,0,1:T(8,128)(2,1)}), bf16[128,2,256]{2,0,1:T(8,128)(2,1)}) %reduce-scatter.2.cloned.1.call-update) | async-done | bytes 131088 | tf_op jit(solution)/shard_map/reduce_scatter | solution.py:22
  604.7 1.0 copy.39
  605.8 2.2 copy.51
  607.9 20.6 %copy.52 = bf16[3072,2,256]{2,1,0:T(2,128)(2,1)} copy(bf16[3072,2,256]{2,0,1:T(8,128)(2,1)S(1)} %bitcast.136) | data formatting | bytes 6291456 | tf_op jit(solution)/shard_map/reshape | solution.py:77
  628.5 6.1 gather_fusion
  634.6 1.3 convert_add_fusion
  635.9 1.6 fusion.92
  637.5 0.6 multiply_reduce_fusion
  638.1 5.8 all_gather.7
  643.8 3.5 fusion.7
  (36 shorter events, 1.7 us)
Async XLA Ops:
  7.4 1.7 copy-start
  50.0 6.5 copy-start.3
  50.0 247.2 %all-to-all-start = ((bf16[8,4,96,1792]{3,2,0,1:T(8,128)(2,1)}), bf16[8,4,96,1792]{3,2,0,1:T(8,128)(2,1)}, u32[]{:S(2)}, u32[]{:S(2)}) async-start(bf16[8,4,96,1792]{3,2,0,1:T(8,128)(2,1)} %copy.42), calls=%async_computation.1 | async-start | bytes 22020096 | tf_op jit(solution)/shard_map/all_to_all | solution.py:41
  56.5 329.0 %all-reduce.4.cloned.1.call-start = ((), (), s32[]{:S(2)}) async-start(), calls=%async_computation.5 | async-start | bytes 6291456 | tf_op jit(solution)/shard_map/psum | solution.py:65
  297.2 5.2 copy-start.5
  317.6 67.9 %copy-start.1 = (bf16[2,960,256]{2,1,0:T(8,128)(2,1)S(1)}, bf16[2,960,256]{2,1,0:T(8,128)(2,1)}, u32[]{:S(2)}) copy-start(bf16[2,960,256]{2,1,0:T(8,128)(2,1)} %param.12) | copy-start | bytes 2949124
  317.6 260.9 %all-gather.2.cloned.1.call-start = ((), (), s32[]{:S(2)}) async-start(), calls=%async_computation.3 | async-start | bytes 13762560 | tf_op jit(solution)/shard_map/all_gather | solution.py:18
  385.4 3.2 copy-start.2
  393.9 211.9 %all-to-all-start.1 = ((bf16[8,4,96,2,256]{4,2,0,3,1:T(8,128)(2,1)}), bf16[8,4,96,2,256]{4,2,0,3,1:T(8,128)(2,1)}, u32[]{:S(2)}, u32[]{:S(2)}) async-start(bf16[8,4,96,2,256]{4,2,0,3,1:T(8,128)(2,1)} %copy.54), calls=%async_computation.2 | async-start | bytes 6291456 | tf_op jit(solution)/shard_map/all_to_all | solution.py:76
  398.5 186.3 %copy-start.4 = (f32[128,8]{0,1:T(8,128)S(1)}, f32[128,8]{0,1:T(8,128)}, u32[]{:S(2)}) copy-start(f32[128,8]{0,1:T(8,128)} %param.9) | copy-start | bytes 12292
  398.5 206.2 %reduce-scatter.2.cloned.1.call-start = ((), (), s32[]{:S(2)}) async-start(), calls=%async_computation.4 | async-start | bytes 655360 | tf_op jit(solution)/shard_map/reduce_scatter | solution.py:22
Sparse Core Ops, SparseCore 0:
  317.7 67.6 all-reduce.3
  584.9 19.7 reduce-scatter.1
Sparse Core Ops, SparseCore 1:
  319.6 258.7 all-gather.1
where the time goes:
time: 664 us; the launch traced here: 655 us
  waiting for transfers between devices  486 us (73%)
  local copies, waits for them, and re-layouts  82.2 us (12%)
  matrix products  31.7 us (5%)
  between operations  30.7 us (5%)
  starting transfers between devices  11.4 us (2%)
  other arithmetic  7.15 us (1%)
    all_to_all x1, waiting for transfers between devices, on_device(): lax.all_to_all(outgoing, 'expert', split_axis=1, concat_axis=1, tiled=True)  219 us
    all_gather x1, waiting for transfers between devices, on_device(): gathered = lax.all_gather(base_weights, 'expert', axis=1, tiled=True)  180 us
    psum x1, waiting for transfers between devices, on_device(): summed = lax.psum(stacked.astype(jnp.bfloat16), ('tensor', 'inner'))  67.2 us
    scatter x1, local copies, waits for them, and re-layouts, on_device(): outgoing = outgoing.at[target].set(tokens[source_row])  31.3 us
    reshape x1, local copies, waits for them, and re-layouts, on_device(): returned.reshape(local_count * owners * capacity, 2, hidden_slice)  20.6 us
    reduce_scatter x1, waiting for transfers between devices, on_device(): lax.psum_scatter(partial_value.astype(jnp.bfloat16), ('tensor', 'inner'),...  19.8 us
    dot_general x8, matrix products, on_device(): lax.dot_general(arrived[member], window, (((1,), (1,)), ((), ())), prefer...  15.2 us
  transfers between devices with their start and end apart: 5, of which 4 were waited for; matrix products, arithmetic and copies ran while one was open for 3% of the time, Pallas kernels for 0%

commit v1 on v0

--- a/solution.py
+++ b/solution.py
@@ -62,7 +62,7 @@
             for member in range(local_count)
         ]
     )
-    summed = lax.psum(stacked.astype(jnp.bfloat16), ("tensor", "inner"))
+    summed = lax.psum(lax.psum(stacked.astype(jnp.bfloat16), "inner"), "tensor")
     latents = [summed[member] for member in range(local_count)]
     outputs = []
     for member in range(local_count):

time: 664 us -> 689 us (1.038)
  waiting for transfers between devices: 486 us -> 511 us
    psum x1 -> x2, waiting for transfers between devices: 67.2 us -> 111 us  [on_device(): summed = lax.psum(lax.psum(stacked.astype(jnp.bfloat16), 'inner'), 'tensor')]
    all_gather x1, waiting for transfers between devices: 180 us -> 160 us  [on_device(): gathered = lax.all_gather(base_weights, 'expert', axis=1, tiled=True)]
  transfers between devices with their start and end apart: 5 -> 6, of which waited for: 4 -> 5; matrix products, arithmetic and copies ran while one was open for 3% -> 3% of each run, Pallas kernels for 0% -> 0%
where the time goes in v1:
time: 689 us; the launch traced here: 680 us
  waiting for transfers between devices  511 us (74%)
  local copies, waits for them, and re-layouts  82.2 us (12%)
  matrix products  31.7 us (5%)
  between operations  30.7 us (4%)
  starting transfers between devices  11.4 us (2%)
  other arithmetic  7.15 us (1%)
    all_to_all x1, waiting for transfers between devices, on_device(): lax.all_to_all(outgoing, 'expert', split_axis=1, concat_axis=1, tiled=True)  219 us
    all_gather x1, waiting for transfers between devices, on_device(): gathered = lax.all_gather(base_weights, 'expert', axis=1, tiled=True)  160 us
    psum x2, waiting for transfers between devices, on_device(): summed = lax.psum(lax.psum(stacked.astype(jnp.bfloat16), 'inner'), 'tensor')  111 us
    scatter x1, local copies, waits for them, and re-layouts, on_device(): outgoing = outgoing.at[target].set(tokens[source_row])  31.3 us
    reshape x1, local copies, waits for them, and re-layouts, on_device(): returned.reshape(local_count * owners * capacity, 2, hidden_slice)  20.6 us
    reduce_scatter x1, waiting for transfers between devices, on_device(): lax.psum_scatter(partial_value.astype(jnp.bfloat16), ('tensor', 'inner'),...  19.7 us
    dot_general x8, matrix products, on_device(): lax.dot_general(arrived[member], window, (((1,), (1,)), ((), ())), prefer...  15.2 us
  transfers between devices with their start and end apart: 6, of which 5 were waited for; matrix products, arithmetic and copies ran while one was open for 3% of the time, Pallas kernels for 0%

profile of v1, /device:TPU:0, one launch (start us, length us, event | category | flops | bytes accessed | tf_op | source)
XLA Modules:
  0.0 679.8 jit_solution(12677376309301847689)
XLA Ops:
  7.4 0.8 copy.40
  8.4 0.5 fusion.52
  9.0 31.3 %scatter_custom_fusion = bf16[3072,1792]{1,0:T(8,128)(2,1)} fusion(s32[1024]{0:T(1024)S(1)} %bitcast.155, bf16[]{:T(256)} %constant.47.clone.1, bf16[128,1792]{1,0:T(8,128)(2,1)S(1)} %copy-done, s32[1024]{0:T(1024)S(1)} %broadcast_clamp_fusion.1), kind=kCustom, calls=%fused_computation.13 | custom fusion | bytes 11010050 | tf_op jit(solution)/shard_map/scatter | solution.py:39
  40.4 9.6 %copy.42 = bf16[8,4,96,1792]{3,2,0,1:T(8,128)(2,1)} copy(bf16[8,4,96,1792]{3,2,1,0:T(8,128)(2,1)} %bitcast.135) | data formatting | bytes 22020096 | tf_op jit(solution)/shard_map/reshape | solution.py:40
  50.0 6.5 all-to-all-start
  56.7 0.7 fusion.94
  72.5 0.7 fusion.93
  73.2 0.6 iota_compare_fusion.15
  73.8 0.6 iota_compare_fusion.14
  74.4 0.6 iota_compare_fusion.13
  75.0 0.7 iota_compare_fusion.12
  75.7 0.6 iota_compare_fusion.11
  76.3 0.7 iota_compare_fusion.10
  77.0 0.6 iota_compare_fusion.9
  77.6 0.7 iota_compare_fusion.8
  78.3 218.9 %all-to-all-done = bf16[8,4,96,1792]{3,2,0,1:T(8,128)(2,1)} async-done(((bf16[8,4,96,1792]{3,2,0,1:T(8,128)(2,1)}), bf16[8,4,96,1792]{3,2,0,1:T(8,128)(2,1)}, u32[]{:S(2)}, u32[]{:S(2)}) %all-to-all-start) | async-done | bytes 11010080 | tf_op jit(solution)/shard_map/all_to_all | solution.py:41
  297.2 4.9 fusion.91
  302.4 1.9 fusion.50
  304.3 1.9 fusion.48
  306.2 1.9 fusion.46
  308.1 1.9 fusion.44
  310.0 1.9 fusion.42
  311.9 1.9 fusion.40
  313.8 1.9 fusion.38
  315.7 1.9 fusion.36
  317.7 22.7 %all-reduce.5.cloned.1.call-done = bf16[8,384,512]{2,1,0:T(8,128)(2,1)} async-done(((bf16[8,384,512]{2,1,0:T(8,128)(2,1)}), bf16[8,384,512]{2,1,0:T(8,128)(2,1)}) %all-reduce.5.cloned.1.call-update) | async-done | bytes 3145744 | tf_op jit(solution)/shard_map/psum | solution.py:65
  340.9 88.7 %all-reduce.7.cloned.1.call-done = bf16[8,384,512]{2,1,0:T(8,128)(2,1)} async-done(((bf16[8,384,512]{2,1,0:T(8,128)(2,1)}), bf16[8,384,512]{2,1,0:T(8,128)(2,1)}) %all-reduce.7.cloned.1.call-update) | async-done | bytes 3145744 | tf_op jit(solution)/shard_map/psum | solution.py:65
  429.7 1.6 convolution_convert_fusion.7
  431.3 1.5 convolution_convert_fusion.6
  432.9 0.5 convolution_convert_fusion.5
  433.5 0.5 convolution_convert_fusion.4
  434.6 0.5 convolution_convert_fusion.2
  435.1 0.5 convolution_convert_fusion.1
  435.7 0.5 convolution_convert_fusion
  436.2 1.9 copy.54
  438.1 4.7 all-to-all-start.1
  442.8 160.3 %all-gather.2.cloned.1.call-done = bf16[3,1024,1792]{2,1,0:T(8,128)(2,1)} async-done(((bf16[3,256,1792]{2,1,0:T(8,128)(2,1)}), bf16[3,1024,1792]{2,1,0:T(8,128)(2,1)}) %all-gather.2.cloned.1.call-update) | async-done | bytes 11010064 | tf_op jit(solution)/shard_map/all_gather | solution.py:18
  603.2 6.3 fusion.16
  609.6 19.7 %reduce-scatter.2.cloned.1.call-done = bf16[128,2,256]{2,0,1:T(8,128)(2,1)} async-done(((bf16[128,2,1024]{2,0,1:T(8,128)(2,1)}), bf16[128,2,256]{2,0,1:T(8,128)(2,1)}) %reduce-scatter.2.cloned.1.call-update) | async-done | bytes 131088 | tf_op jit(solution)/shard_map/reduce_scatter | solution.py:22
  629.4 1.0 copy.39
  630.4 2.2 copy.51
  632.6 20.6 %copy.52 = bf16[3072,2,256]{2,1,0:T(2,128)(2,1)} copy(bf16[3072,2,256]{2,0,1:T(8,128)(2,1)S(1)} %bitcast.136) | data formatting | bytes 6291456 | tf_op jit(solution)/shard_map/reshape | solution.py:77
  653.2 6.1 gather_fusion
  659.2 1.3 convert_add_fusion
  660.5 1.6 fusion.92
  662.1 0.6 multiply_reduce_fusion
  662.7 5.8 all_gather.7
  668.5 3.5 fusion.7
  (39 shorter events, 2.3 us)
Async XLA Ops:
  7.4 1.7 copy-start
  50.0 6.5 copy-start.3
  50.0 247.2 %all-to-all-start = ((bf16[8,4,96,1792]{3,2,0,1:T(8,128)(2,1)}), bf16[8,4,96,1792]{3,2,0,1:T(8,128)(2,1)}, u32[]{:S(2)}, u32[]{:S(2)}) async-start(bf16[8,4,96,1792]{3,2,0,1:T(8,128)(2,1)} %copy.42), calls=%async_computation.1 | async-start | bytes 22020096 | tf_op jit(solution)/shard_map/all_to_all | solution.py:41
  56.5 283.8 %all-reduce.5.cloned.1.call-start = ((), (), s32[]{:S(2)}) async-start(), calls=%async_computation.5 | async-start | bytes 6291456 | tf_op jit(solution)/shard_map/psum | solution.py:65
  297.2 5.2 copy-start.5
  317.6 112.0 %copy-start.1 = (bf16[2,960,256]{2,1,0:T(8,128)(2,1)S(1)}, bf16[2,960,256]{2,1,0:T(8,128)(2,1)}, u32[]{:S(2)}) copy-start(bf16[2,960,256]{2,1,0:T(8,128)(2,1)} %param.12) | copy-start | bytes 2949124
  317.6 112.0 %all-reduce.7.cloned.1.call-start = ((), (), s32[]{:S(2)}) async-start(), calls=%async_computation.6 | async-start | bytes 6291456 | tf_op jit(solution)/shard_map/psum | solution.py:65
  340.4 262.8 %all-gather.2.cloned.1.call-start = ((), (), s32[]{:S(2)}) async-start(), calls=%async_computation.3 | async-start | bytes 13762560 | tf_op jit(solution)/shard_map/all_gather | solution.py:18
  429.7 3.2 copy-start.2
  438.1 192.3 %all-to-all-start.1 = ((bf16[8,4,96,2,256]{4,2,0,3,1:T(8,128)(2,1)}), bf16[8,4,96,2,256]{4,2,0,3,1:T(8,128)(2,1)}, u32[]{:S(2)}, u32[]{:S(2)}) async-start(bf16[8,4,96,2,256]{4,2,0,3,1:T(8,128)(2,1)} %copy.54), calls=%async_computation.2 | async-start | bytes 6291456 | tf_op jit(solution)/shard_map/all_to_all | solution.py:76
  442.8 166.7 %copy-start.4 = (f32[128,8]{0,1:T(8,128)S(1)}, f32[128,8]{0,1:T(8,128)}, u32[]{:S(2)}) copy-start(f32[128,8]{0,1:T(8,128)} %param.9) | copy-start | bytes 12292
  442.8 186.6 %reduce-scatter.2.cloned.1.call-start = ((), (), s32[]{:S(2)}) async-start(), calls=%async_computation.4 | async-start | bytes 655360 | tf_op jit(solution)/shard_map/reduce_scatter | solution.py:22
Sparse Core Ops, SparseCore 0:
  317.7 22.5 all-reduce.4
  342.6 86.9 all-reduce.6
Sparse Core Ops, SparseCore 1:
  342.4 260.7 all-gather.1
  609.6 19.7 reduce-scatter.1
